TPU v7x, 32 devices: a whole 2x2x4 slice. The times are simulated.
32 devices in a mesh: tile: 8 (over z, y), view: 4 (over x, core).
Axes of the slice: x: 2, y: 2, z: 4, core: 2. Of those that a mesh axis runs over, the one named last changes fastest.
Arguments:
- recorded: bfloat16 [4, 128, 256, 256], P('view', 'tile'), may hold values from 0.099609375 to 10
- estimate: float32 [128, 256, 256], P('tile', 'view'), may hold values from 0.5 to 2
- psf_taps: float32 [16, 3, 31], replicated, may hold values from 0.05 to 1
- half_width: int32 [16, 3], replicated, may hold values from 8 to 15
- assign: int32 [4], replicated, may hold values from 0 to 15
- flags: int32 [16, 32], P('tile', 'view'), may hold values 0 or 1
Outputs:
- restored: float32 [128, 256, 256], P('tile', 'view')
All inputs are finite; a program needn't handle non-finite values. No bound on the sum of `flags` on one device may be relied on, other than what follows from the above.
Results may differ from a plain program's by a relative error of at most 0.0007.
Values may be sent and summed in bfloat16 or wider, within the bound.
A program may use at most 64 MiB of HBM per device.

v0:
```python
import jax
import jax.numpy as jnp
from jax import lax
from jax.sharding import PartitionSpec as P

VIEWS = 4
KERNELS = 16
TAPS = 31


def padded_2(cells, sides, width):
    for axis, dim in sides:
        count = lax.axis_size(axis)
        ends = count - 1
        head = lax.slice_in_dim(cells, 0, width, axis=dim)
        tail = lax.slice_in_dim(cells, cells.shape[dim] - width, cells.shape[dim], axis=dim)
        cells = jnp.concatenate(
            [
                lax.ppermute(tail, axis, [(i, (i + 1) % count) for i in range(ends)]),
                cells,
                lax.ppermute(head, axis, [((i + 1) % count, i) for i in range(ends)]),
            ],
            axis=dim,
        )
    return cells


def make_kernels(psf_taps, half_width, assign):
    offsets = jnp.abs(jnp.arange(TAPS) - TAPS // 2)
    keep = (offsets[None, None, :] <= half_width[:, :, None]).astype(jnp.float32)
    raw = psf_taps * keep
    kern = raw / jnp.sum(raw, axis=-1, keepdims=True)
    picker = (assign[:, None] == jnp.arange(KERNELS)[None, :]).astype(jnp.float32)
    return jnp.einsum("sv,vaj->saj", picker, kern, precision=lax.Precision.HIGHEST)


def band_matrix(kernel, rows_count, cols_count, shift):
    rows = jnp.arange(rows_count)[:, None]
    cols = jnp.arange(cols_count)[None, :]
    offset = rows - cols + shift
    hits = (offset[None, :, :] == jnp.arange(TAPS)[:, None, None]).astype(jnp.float32)
    return jnp.sum(kernel[:, None, None] * hits, axis=0)


def along_second(volume, band):
    return jnp.einsum("xpz,pi->xiz", volume, band, precision=lax.Precision.HIGHEST)


def along_third(volume, band):
    return jnp.einsum("xyp,pi->xyi", volume, band, precision=lax.Precision.HIGHEST)


def shards(recorded, estimate, psf_taps, half_width, assign, flags):
    slab = estimate.shape[0]
    full_y = recorded.shape[2]
    depth_z = recorded.shape[3]
    kernels = make_kernels(psf_taps, half_width, assign)
    flipped = kernels[:, :, ::-1]
    slot = lax.axis_index("view")
    selector = (jnp.arange(VIEWS) == slot).astype(jnp.float32)
    own_kern = jnp.einsum("s,saj->aj", selector, kernels, precision=lax.Precision.HIGHEST)
    own_flip = jnp.einsum("s,saj->aj", selector, flipped, precision=lax.Precision.HIGHEST)
    padded_rows = slab + TAPS - 1
    first_own_flip = band_matrix(own_flip[0], padded_rows, slab, 0)
    second_own = band_matrix(own_kern[1], full_y, full_y, TAPS // 2)
    third_own = band_matrix(own_kern[2], depth_z, depth_z, TAPS // 2)
    second_flip = band_matrix(own_flip[1], full_y, full_y, TAPS // 2)
    third_flip = band_matrix(own_flip[2], depth_z, depth_z, TAPS // 2)
    first_all = jnp.stack([band_matrix(kernels[s, 0], padded_rows, slab, 0) for s in range(VIEWS)])
    cells = jnp.repeat(jnp.repeat(flags, 8, axis=0), 8, axis=1)[:, :, None] > 0
    data_slab = recorded[0].astype(jnp.float32)
    current = estimate
    rounded = current.astype(jnp.bfloat16)
    padded = padded_2(rounded, (("tile", 0),), TAPS // 2).astype(jnp.float32)
    stacked = jnp.einsum("pyz,spi->siyz", padded, first_all, precision=lax.Precision.HIGHEST)
    first_pass = lax.all_to_all(
        stacked.astype(jnp.bfloat16), "view", split_axis=0, concat_axis=2, tiled=True
    ).astype(stacked.dtype)[0]
    blurred = along_third(along_second(first_pass, second_own), third_own)
    ratio = (data_slab / blurred).astype(jnp.bfloat16)
    padded_ratio = padded_2(ratio, (("tile", 0),), TAPS // 2).astype(jnp.float32)
    back = jnp.einsum("pyz,pi->iyz", padded_ratio, first_own_flip, precision=lax.Precision.HIGHEST)
    back = along_third(along_second(back, second_flip), third_flip)
    total = lax.psum_scatter(back, "view", scatter_dimension=1, tiled=True)
    correction = total / VIEWS
    current = jnp.where(cells, current * correction, current)
    return current


def solution(mesh):
    placed = (
        P("view", "tile", None, None),
        P("tile", "view", None),
        P(),
        P(),
        P(),
        P("tile", "view"),
    )
    return jax.shard_map(
        shards, mesh=mesh, in_specs=placed, out_specs=P("tile", "view", None), check_vma=False
    )
```

profile of v0, /device:TPU:21, one launch (start us, length us, event | category | flops | bytes accessed | tf_op | source)
XLA Modules:
  0.0 234.7 jit_solution(3409513282182263963)
XLA Ops:
  6.5 1.8 copy.35
  8.6 3.1 %collective-permute-start = (bf16[15,64,256]{2,0,1:T(8,128)(2,1)S(1)}, bf16[15,64,256]{2,0,1:T(8,128)(2,1)S(1)}, u32[]{:S(2)}, u32[]{:S(2)}) collective-permute-start(bf16[15,64,256]{2,0,1:T(8,128)(2,1)S(1)} %get-tuple-element.16), channel_id=1, source_target_pairs={{0,4},{4,8},{8,12},{12,16},{16,20},{20,24},{24,28},{1,5},{5,9},{9,... | collective-permute-start | bytes 1474568 | tf_op jit(solution)/shard_map/ppermute | solution.py:19
  11.7 2.1 collective-permute-start.1
  13.9 0.9 fusion.29
  14.8 0.9 fusion.27
  16.4 18.1 %collective-permute-done = bf16[15,64,256]{2,0,1:T(8,128)(2,1)S(1)} collective-permute-done((bf16[15,64,256]{2,0,1:T(8,128)(2,1)S(1)}, bf16[15,64,256]{2,0,1:T(8,128)(2,1)S(1)}, u32[]{:S(2)}, u32[]{:S(2)}) %collective-permute-start) | collective-permute-done | bytes 491552 | tf_op jit(solution)/shard_map/ppermute | solution.py:19
  34.5 3.2 %convolution_convert_fusion = bf16[4,16,64,256]{3,1,2,0:T(8,128)(2,1)} fusion(bf16[15,64,256]{2,0,1:T(8,128)(2,1)S(1)} %collective-permute-done.1, bf16[16,64,256]{2,0,1:T(8,128)(2,1)S(1)} %copy.35, bf16[15,64,256]{2,0,1:T(8,128)(2,1)S(1)} %collective-permute-done, f32[1,46,16]{1,2,0:T(8,128)S(1)} %bitcast.83, f32[1,46,16]{1,2,0:T(8,128)S(1)} %bitcast.84, ...), kind=kOutput, calls=%fused_computation.18 | convolution fusion | flops 584393344 | bytes 3616256 | tf_op jit(solution)/shard_map/pyz,spi->siyz/dot_general | solution.py:75
  37.7 5.1 %all-to-all-start = ((bf16[4,16,64,256]{3,1,2,0:T(8,128)(2,1)}), bf16[4,16,64,256]{3,1,2,0:T(8,128)(2,1)S(1)}, u32[]{:S(2)}, u32[]{:S(2)}) async-start(bf16[4,16,64,256]{3,1,2,0:T(8,128)(2,1)} %convolution_convert_fusion), calls=%async_computation | async-start | bytes 4194304 | tf_op jit(solution)/shard_map/all_to_all | solution.py:76
  42.8 3.6 %select_reduce_fusion = (f32[256,256]{1,0:T(8,128)S(1)}, f32[256,256]{1,0:T(8,128)S(1)}, f32[256,256]{1,0:T(8,128)S(1)}, f32[256,256]{1,0:T(8,128)S(1)}) fusion(f32[31]{0:T(128)S(1)} %get-tuple-element.28, s32[256,256]{1,0:T(8,128)S(1)} %subtract_add_fusion, f32[31]{0:T(128)S(1)} %get-tuple-element.26, f32[31]{0:T(128)S(1)} %get-tuple-element.25, ...), kind=kLoop, calls=%fused_computation | loop fusion | flops 18022400 | bytes 1311216 | tf_op jit(solution)/shard_map/reduce_sum | solution.py:42
  46.4 21.0 %all-to-all-done = bf16[4,16,64,256]{3,1,2,0:T(8,128)(2,1)S(1)} async-done(((bf16[4,16,64,256]{3,1,2,0:T(8,128)(2,1)}), bf16[4,16,64,256]{3,1,2,0:T(8,128)(2,1)S(1)}, u32[]{:S(2)}, u32[]{:S(2)}) %all-to-all-start) | async-done | bytes 2097184 | tf_op jit(solution)/shard_map/all_to_all | solution.py:76
  67.5 2.2 fusion.9
  69.7 3.7 %fusion.2 = bf16[16,256,256]{2,1,0:T(8,128)(2,1)S(1)} fusion(bf16[1,16,256,256]{3,2,1,0:T(8,128)(2,1)S(1)} %copy-done.1, f32[256,16,256]{2,0,1:T(8,128)S(1)} %fusion.9, f32[256,256]{1,0:T(8,128)S(1)} %get-tuple-element.6), kind=kOutput, calls=%fused_computation.9 | convolution fusion | flops 3224371200 | bytes 8650752 | tf_op jit(solution)/shard_map/xyp,pi->xyi/dot_general | solution.py:50
  73.3 0.4 fusion.51
  73.8 4.0 %collective-permute-start.2 = (bf16[15,256,256]{2,1,0:T(8,128)(2,1)S(1)}, bf16[15,256,256]{2,1,0:T(8,128)(2,1)S(1)}, u32[]{:S(2)}, u32[]{:S(2)}) collective-permute-start(bf16[15,256,256]{2,1,0:T(8,128)(2,1)S(1)} %get-tuple-element.14), channel_id=1, source_target_pairs={{0,4},{4,8},{8,12},{12,16},{16,20},{20,24},{24,28},{1,5},{5,9},{9,... | collective-permute-start | bytes 5898248 | tf_op jit(solution)/shard_map/ppermute | solution.py:19
  77.8 2.1 collective-permute-start.3
  79.9 81.3 %collective-permute-done.2 = bf16[15,256,256]{2,1,0:T(8,128)(2,1)S(1)} collective-permute-done((bf16[15,256,256]{2,1,0:T(8,128)(2,1)S(1)}, bf16[15,256,256]{2,1,0:T(8,128)(2,1)S(1)}, u32[]{:S(2)}, u32[]{:S(2)}) %collective-permute-start.2) | collective-permute-done | bytes 1966112 | tf_op jit(solution)/shard_map/ppermute | solution.py:19
  161.2 1.2 collective-permute-done.3
  162.4 0.9 pad_maximum_fusion
  163.3 5.3 %fusion = f32[16,256,256]{2,0,1:T(8,128)S(1)} fusion(bf16[46,256,256]{2,1,0:T(8,128)(2,1)S(1)} %pad_maximum_fusion, f32[46,16]{0,1:T(8,128)S(1)} %get-tuple-element.9), kind=kOutput, calls=%fused_computation.5 | convolution fusion | flops 578813952 | bytes 10226560 | tf_op jit(solution)/shard_map/pyz,pi->iyz/dot_general | solution.py:82
  168.6 6.2 %fusion.7 = f32[256,16,256]{2,0,1:T(8,128)S(1)} fusion(f32[16,256,256]{2,0,1:T(8,128)S(1)} %fusion, f32[256,256]{1,0:T(8,128)S(1)} %get-tuple-element.8), kind=kOutput, calls=%fused_computation.14 | convolution fusion | flops 3221225472 | bytes 8650752 | tf_op jit(solution)/shard_map/xpz,pi->xiz/dot_general | solution.py:46
  174.8 5.0 %fusion.3 = f32[16,256,256]{2,1,0:T(8,128)} fusion(f32[256,16,256]{2,0,1:T(8,128)S(1)} %fusion.7, f32[256,256]{1,0:T(8,128)S(1)} %get-tuple-element.5), kind=kOutput, calls=%fused_computation.10 | convolution fusion | flops 3221225472 | bytes 8650752 | tf_op jit(solution)/shard_map/xyp,pi->xyi/dot_general | solution.py:50
  179.8 0.7 copy-done.2
  180.7 44.8 %reduce-scatter.2.cloned.1.call-done = f32[16,64,256]{2,1,0:T(8,128)} async-done(((f32[16,256,256]{2,1,0:T(8,128)}), f32[16,64,256]{2,1,0:T(8,128)}) %reduce-scatter.2.cloned.1.call-update) | async-done | bytes 1048592 | tf_op jit(solution)/shard_map/reduce_scatter | solution.py:84
  225.4 2.4 %multiply_select_fusion = f32[16,64,256]{2,1,0:T(8,128)} fusion(f32[16,64,256]{2,1,0:T(8,128)S(1)} %copy-done, f32[16,64,256]{2,1,0:T(8,128)} %reduce-scatter.2.cloned.1.call-done, pred[16,64]{1,0:T(8,128)(4,1)S(1)} %copy.12), kind=kLoop, calls=%fused_computation.24 | loop fusion | flops 786432 | bytes 3146752 | tf_op jit(solution)/shard_map/jit(_where)/select_n | solution.py:86
  (25 shorter events, 1.1 us)
Async XLA Ops:
  8.6 25.9 %collective-permute-start = (bf16[15,64,256]{2,0,1:T(8,128)(2,1)S(1)}, bf16[15,64,256]{2,0,1:T(8,128)(2,1)S(1)}, u32[]{:S(2)}, u32[]{:S(2)}) collective-permute-start(bf16[15,64,256]{2,0,1:T(8,128)(2,1)S(1)} %get-tuple-element.16), channel_id=1, source_target_pairs={{0,4},{4,8},{8,12},{12,16},{16,20},{20,24},{24,28},{1,5},{5,9},{9,... | collective-permute-start | bytes 1474568 | tf_op jit(solution)/shard_map/ppermute | solution.py:19
  11.7 22.8 %collective-permute-start.1 = (bf16[15,64,256]{2,0,1:T(8,128)(2,1)S(1)}, bf16[15,64,256]{2,0,1:T(8,128)(2,1)S(1)}, u32[]{:S(2)}, u32[]{:S(2)}) collective-permute-start(bf16[15,64,256]{2,0,1:T(8,128)(2,1)S(1)} %get-tuple-element.17), channel_id=1, source_target_pairs={{4,0},{8,4},{12,8},{16,12},{20,16},{24,20},{28,24},{5,1},{9,5},{13... | collective-permute-start | bytes 1474568 | tf_op jit(solution)/shard_map/ppermute | solution.py:21
  37.7 29.8 %all-to-all-start = ((bf16[4,16,64,256]{3,1,2,0:T(8,128)(2,1)}), bf16[4,16,64,256]{3,1,2,0:T(8,128)(2,1)S(1)}, u32[]{:S(2)}, u32[]{:S(2)}) async-start(bf16[4,16,64,256]{3,1,2,0:T(8,128)(2,1)} %convolution_convert_fusion), calls=%async_computation | async-start | bytes 4194304 | tf_op jit(solution)/shard_map/all_to_all | solution.py:76
  42.8 182.7 %reduce-scatter.2.cloned.1.call-start = ((), (), s32[]{:S(2)}) async-start(), calls=%async_computation.2 | async-start | bytes 5242880 | tf_op jit(solution)/shard_map/reduce_scatter | solution.py:84
  67.5 2.2 copy-start.1
  73.8 87.4 %collective-permute-start.2 = (bf16[15,256,256]{2,1,0:T(8,128)(2,1)S(1)}, bf16[15,256,256]{2,1,0:T(8,128)(2,1)S(1)}, u32[]{:S(2)}, u32[]{:S(2)}) collective-permute-start(bf16[15,256,256]{2,1,0:T(8,128)(2,1)S(1)} %get-tuple-element.14), channel_id=1, source_target_pairs={{0,4},{4,8},{8,12},{12,16},{16,20},{20,24},{24,28},{1,5},{5,9},{9,... | collective-permute-start | bytes 5898248 | tf_op jit(solution)/shard_map/ppermute | solution.py:19
  77.8 84.5 %collective-permute-start.3 = (bf16[15,256,256]{2,1,0:T(8,128)(2,1)S(1)}, bf16[15,256,256]{2,1,0:T(8,128)(2,1)S(1)}, u32[]{:S(2)}, u32[]{:S(2)}) collective-permute-start(bf16[15,256,256]{2,1,0:T(8,128)(2,1)S(1)} %get-tuple-element.15), channel_id=1, source_target_pairs={{4,0},{8,4},{12,8},{16,12},{20,16},{24,20},{28,24},{5,1},{9,5},{13... | collective-permute-start | bytes 5898248 | tf_op jit(solution)/shard_map/ppermute | solution.py:21
  179.8 0.7 copy-start.2
  179.8 45.6 %copy-start = (f32[16,64,256]{2,1,0:T(8,128)S(1)}, f32[16,64,256]{2,1,0:T(8,128)}, u32[]{:S(2)}) copy-start(f32[16,64,256]{2,1,0:T(8,128)} %param.7) | copy-start | bytes 3145732
Sparse Core Ops, SparseCore 0:
  179.9 45.4 reduce-scatter.1
where the time goes:
time: 237 us; the launch traced here: 235 us
  waiting for transfers between devices  166 us (70%)
  matrix products  26.7 us (11%)
  starting transfers between devices  16.5 us (7%)
  between operations  13.6 us (6%)
  other arithmetic  8.14 us (3%)
  local copies, waits for them, and re-layouts  3.41 us (1%)
    ppermute x2, waiting for transfers between devices, padded_2(): lax.ppermute(tail, axis, [(i, (i + 1) % count) for i in range(ends)])  99.4 us
    reduce_scatter x1, waiting for transfers between devices, shards(): total = lax.psum_scatter(back, 'view', scatter_dimension=1, tiled=True)  44.8 us
    all_to_all x1, waiting for transfers between devices, shards(): lax.all_to_all(stacked.astype(jnp.bfloat16), 'view', split_axis=0, concat...  21 us
    dot_general x2, matrix products, along_third(): jnp.einsum('xyp,pi->xyi', volume, band, precision=lax.Precision.HIGHEST)  8.62 us
    dot_general x2, matrix products, along_second(): jnp.einsum('xpz,pi->xiz', volume, band, precision=lax.Precision.HIGHEST)  8.44 us
    ppermute x2, starting transfers between devices, padded_2(): lax.ppermute(tail, axis, [(i, (i + 1) % count) for i in range(ends)])  7.19 us
    dot_general x1, matrix products, shards(): jnp.einsum('pyz,pi->iyz', padded_ratio, first_own_flip, precision=lax.Pre...  5.27 us
    all_to_all x1, starting transfers between devices, shards(): lax.all_to_all(stacked.astype(jnp.bfloat16), 'view', split_axis=0, concat...  5.1 us
  transfers between devices with their start and end apart: 6, of which 5 were waited for; matrix products, arithmetic and copies ran while one was open for 3% of the time, Pallas kernels for 0%

commit v1 on v0

v1 whole, which is shorter than its diff:
```python
import jax
import jax.numpy as jnp
from jax import lax
from jax.sharding import PartitionSpec as P

VIEWS = 4
KERNELS = 16
TAPS = 31
HALF = TAPS // 2
HIGH = lax.Precision.HIGH


def make_kernels(psf_taps, half_width, assign):
    offsets = jnp.abs(jnp.arange(TAPS) - HALF)
    keep = (offsets[None, None, :] <= half_width[:, :, None]).astype(jnp.float32)
    raw = psf_taps * keep
    kern = raw / jnp.sum(raw, axis=-1, keepdims=True)
    picker = (assign[:, None] == jnp.arange(KERNELS)[None, :]).astype(jnp.float32)
    return jnp.einsum("sv,vaj->saj", picker, kern, precision=lax.Precision.HIGHEST)


def band_matrix(kernel, rows_count, cols_count, shift):
    rows = jnp.arange(rows_count)[:, None]
    cols = jnp.arange(cols_count)[None, :]
    offset = rows - cols + shift
    hits = (offset[None, :, :] == jnp.arange(TAPS)[:, None, None]).astype(jnp.float32)
    return jnp.sum(kernel[:, None, None] * hits, axis=0)


def shards(recorded, estimate, psf_taps, half_width, assign, flags):
    slab = estimate.shape[0]
    full_y = recorded.shape[2]
    depth_z = recorded.shape[3]
    count = lax.axis_size("tile")
    up = [(i, i + 1) for i in range(count - 1)]
    down = [(i + 1, i) for i in range(count - 1)]
    kernels = make_kernels(psf_taps, half_width, assign)
    slot = lax.axis_index("view")
    selector = (jnp.arange(VIEWS) == slot).astype(jnp.float32)
    own_kern = jnp.einsum("s,saj->aj", selector, kernels, precision=lax.Precision.HIGHEST)
    second_own = band_matrix(own_kern[1], full_y, full_y, HALF)
    third_own = band_matrix(own_kern[2], depth_z, depth_z, HALF)
    padded_rows = slab + TAPS - 1
    first_all = jnp.stack([band_matrix(kernels[s, 0], padded_rows, slab, 0) for s in range(VIEWS)])
    cells = jnp.repeat(jnp.repeat(flags, 8, axis=0), 8, axis=1)[:, :, None] > 0
    rounded = estimate.astype(jnp.bfloat16)
    padded = jnp.concatenate(
        [
            lax.ppermute(rounded[slab - HALF:], "tile", up),
            rounded,
            lax.ppermute(rounded[:HALF], "tile", down),
        ],
        axis=0,
    ).astype(jnp.float32)
    stacked = jnp.einsum("pyz,spi->siyz", padded, first_all, precision=HIGH)
    first_pass = lax.all_to_all(
        stacked.astype(jnp.bfloat16), "view", split_axis=0, concat_axis=2, tiled=True
    )[0].astype(jnp.float32)
    blurred = jnp.einsum("xpz,pi->xiz", first_pass, second_own, precision=HIGH)
    blurred = jnp.einsum("xyp,pi->xyi", blurred, third_own, precision=HIGH)
    ratio = (recorded[0].astype(jnp.float32) / blurred).astype(jnp.bfloat16).astype(jnp.float32)
    back = jnp.einsum("xpz,ip->xiz", ratio, second_own, precision=HIGH)
    back = jnp.einsum("xyp,ip->xyi", back, third_own, precision=HIGH)
    parts = lax.all_to_all(
        back.astype(jnp.bfloat16)[None], "view", split_axis=2, concat_axis=0, tiled=True
    ).astype(jnp.float32)
    wide = jnp.einsum("spyz,sip->iyz", parts, first_all, precision=HIGH)
    spread = wide.astype(jnp.bfloat16)
    below = lax.ppermute(spread[slab + HALF:], "tile", up).astype(jnp.float32)
    above = lax.ppermute(spread[:HALF], "tile", down).astype(jnp.float32)
    total = wide[HALF:slab + HALF]
    total = total + jnp.pad(below, ((0, slab - HALF), (0, 0), (0, 0)))
    total = total + jnp.pad(above, ((slab - HALF, 0), (0, 0), (0, 0)))
    correction = total / VIEWS
    return jnp.where(cells, estimate * correction, estimate)


def solution(mesh):
    placed = (
        P("view", "tile", None, None),
        P("tile", "view", None),
        P(),
        P(),
        P(),
        P("tile", "view"),
    )
    return jax.shard_map(
        shards, mesh=mesh, in_specs=placed, out_specs=P("tile", "view", None), check_vma=False
    )
```

time: 237 us -> 132 us (0.56)
  waiting for transfers between devices: 166 us -> 64.1 us
  blocking collectives: 0 us -> 28.1 us
  matrix products: 26.7 us -> 10.9 us
  between operations: 13.6 us -> 0.2 us
  other arithmetic: 8.14 us -> 4.15 us
  local copies, waits for them, and re-layouts: 3.41 us -> 6.14 us
    ppermute x4, waiting for transfers between devices: 101 us -> 41 us  [the longest x1 20 us: shards(): lax.ppermute(rounded[slab - HALF:], 'tile', up)]
    reduce_scatter x1 -> x0, waiting for transfers between devices: 44.8 us -> none  [shards(): total = lax.psum_scatter(back, 'view', scatter_dimension=1, tiled=True)]
    all_to_all x0 -> x1, blocking collectives: none -> 28.1 us  [shards(): lax.all_to_all(back.astype(jnp.bfloat16)[None], 'view', split_axis=2, con...]
    dot_general x7 -> x6, matrix products: 25.6 us -> 10.5 us  [the longest x1 2.59 us: shards(): stacked = jnp.einsum('pyz,spi->siyz', padded, first_all, precision=HIGH)]
  transfers between devices with their start and end apart: 6 -> 5, of which waited for: 5 -> 4; matrix products, arithmetic and copies ran while one was open for 3% -> 2% of each run, Pallas kernels for 0% -> 0%
where the time goes in v1:
time: 132 us; the launch traced here: 130 us
  waiting for transfers between devices  64.1 us (49%)
  blocking collectives  28.1 us (21%)
  starting transfers between devices  16.3 us (12%)
  matrix products  10.9 us (8%)
  local copies, waits for them, and re-layouts  6.14 us (5%)
  other arithmetic  4.15 us (3%)
    all_to_all x1, blocking collectives, shards(): lax.all_to_all(back.astype(jnp.bfloat16)[None], 'view', split_axis=2, con...  28.1 us
    all_to_all x1, waiting for transfers between devices, shards(): lax.all_to_all(stacked.astype(jnp.bfloat16), 'view', split_axis=0, concat...  23.1 us
    ppermute x1, waiting for transfers between devices, shards(): lax.ppermute(rounded[slab - HALF:], 'tile', up)  20 us
    ppermute x1, waiting for transfers between devices, shards(): below = lax.ppermute(spread[slab + HALF:], 'tile', up).astype(jnp.float32)  19.8 us
    all_to_all x1, starting transfers between devices, shards(): lax.all_to_all(stacked.astype(jnp.bfloat16), 'view', split_axis=0, concat...  5.11 us
    ppermute x1, starting transfers between devices, shards(): below = lax.ppermute(spread[slab + HALF:], 'tile', up).astype(jnp.float32)  4.03 us
    ppermute x1, starting transfers between devices, shards(): lax.ppermute(rounded[slab - HALF:], 'tile', up)  3.15 us
  transfers between devices with their start and end apart: 5, of which 4 were waited for; matrix products, arithmetic and copies ran while one was open for 2% of the time, Pallas kernels for 0%

profile of v1, /device:TPU:21, one launch (start us, length us, event | category | flops | bytes accessed | tf_op | source)
XLA Modules:
  0.0 129.9 jit_solution(4638276544943994386)
XLA Ops:
  0.0 1.8 %copy.57 = bf16[16,64,256]{2,0,1:T(8,128)(2,1)S(1)} copy(f32[16,64,256]{2,1,0:T(8,128)} %param.7) | data formatting | bytes 1572864 | tf_op args[1]
  1.8 0.2 fusion.49
  2.1 3.1 %collective-permute-start = (bf16[15,64,256]{2,0,1:T(8,128)(2,1)S(1)}, bf16[15,64,256]{2,0,1:T(8,128)(2,1)S(1)}, u32[]{:S(2)}, u32[]{:S(2)}) collective-permute-start(bf16[15,64,256]{2,0,1:T(8,128)(2,1)S(1)} %get-tuple-element.13), channel_id=1, source_target_pairs={{0,4},{4,8},{8,12},{12,16},{16,20},{20,24},{24,28},{1,5},{5,9},{9,... | collective-permute-start | bytes 1474568 | tf_op jit(solution)/shard_map/ppermute | solution.py:49
  5.2 2.1 %collective-permute-start.1 = (bf16[15,64,256]{2,0,1:T(8,128)(2,1)S(1)}, bf16[15,64,256]{2,0,1:T(8,128)(2,1)S(1)}, u32[]{:S(2)}, u32[]{:S(2)}) collective-permute-start(bf16[15,64,256]{2,0,1:T(8,128)(2,1)S(1)} %get-tuple-element.14), channel_id=1, source_target_pairs={{4,0},{8,4},{12,8},{16,12},{20,16},{24,20},{28,24},{5,1},{9,5},{13... | collective-permute-start | bytes 1474568 | tf_op jit(solution)/shard_map/ppermute | solution.py:51
  7.6 0.2 fusion.29
  8.0 20.0 %collective-permute-done = bf16[15,64,256]{2,0,1:T(8,128)(2,1)S(1)} collective-permute-done((bf16[15,64,256]{2,0,1:T(8,128)(2,1)S(1)}, bf16[15,64,256]{2,0,1:T(8,128)(2,1)S(1)}, u32[]{:S(2)}, u32[]{:S(2)}) %collective-permute-start) | collective-permute-done | bytes 491552 | tf_op jit(solution)/shard_map/ppermute | solution.py:49
  28.0 2.6 %convolution_convert_fusion = bf16[4,16,64,256]{3,1,2,0:T(8,128)(2,1)} fusion(bf16[15,64,256]{2,0,1:T(8,128)(2,1)S(1)} %collective-permute-done.1, bf16[16,64,256]{2,0,1:T(8,128)(2,1)S(1)} %copy.57, bf16[15,64,256]{2,0,1:T(8,128)(2,1)S(1)} %collective-permute-done, f32[1,46,16]{1,2,0:T(8,128)S(1)} %bitcast.89, f32[1,46,16]{1,2,0:T(8,128)S(1)} %bitcast.91, ...), kind=kOutput, calls=%fused_computation.16 | convolution fusion | flops 294986368 | bytes 3616256 | tf_op jit(solution)/shard_map/pyz,spi->siyz/dot_general | solution.py:55
  30.6 5.1 %all-to-all-start = ((bf16[4,16,64,256]{3,1,2,0:T(8,128)(2,1)}), bf16[4,16,64,256]{3,1,2,0:T(8,128)(2,1)S(1)}, u32[]{:S(2)}, u32[]{:S(2)}) async-start(bf16[4,16,64,256]{3,1,2,0:T(8,128)(2,1)} %convolution_convert_fusion), calls=%async_computation | async-start | bytes 4194304 | tf_op jit(solution)/shard_map/all_to_all | solution.py:56
  35.9 1.4 %select_reduce_fusion = (f32[256,256]{1,0:T(8,128)S(1)}, f32[256,256]{1,0:T(8,128)S(1)}) fusion(f32[31]{0:T(128)S(1)} %get-tuple-element.20, s32[256,256]{1,0:T(8,128)S(1)} %subtract_add_fusion, f32[31]{0:T(128)S(1)} %get-tuple-element.19), kind=kLoop, calls=%fused_computation | loop fusion | flops 10027008 | bytes 786680 | tf_op jit(solution)/shard_map/reduce_sum | solution.py:27
  37.3 23.1 %all-to-all-done = bf16[4,16,64,256]{3,1,2,0:T(8,128)(2,1)S(1)} async-done(((bf16[4,16,64,256]{3,1,2,0:T(8,128)(2,1)}), bf16[4,16,64,256]{3,1,2,0:T(8,128)(2,1)S(1)}, u32[]{:S(2)}, u32[]{:S(2)}) %all-to-all-start) | async-done | bytes 2097184 | tf_op jit(solution)/shard_map/all_to_all | solution.py:56
  60.4 1.7 %fusion.8 = f32[256,16,256]{2,0,1:T(8,128)S(1)} fusion(bf16[16,256,256]{2,0,1:T(8,128)(2,1)S(1)} %bitcast.85, f32[256,256]{1,0:T(8,128)S(1)} %get-tuple-element.6), kind=kOutput, calls=%fused_computation.12 | convolution fusion | flops 1610612736 | bytes 6553600 | tf_op jit(solution)/shard_map/xpz,pi->xiz/dot_general | solution.py:59
  62.2 1.9 %fusion.3 = f32[16,256,256]{2,1,0:T(8,128)S(1)} fusion(f32[256,16,256]{2,0,1:T(8,128)S(1)} %fusion.8, f32[256,256]{1,0:T(8,128)S(1)} %get-tuple-element.5), kind=kOutput, calls=%fused_computation.7 | convolution fusion | flops 1610612736 | bytes 8650752 | tf_op jit(solution)/shard_map/xyp,pi->xyi/dot_general | solution.py:60
  64.1 1.4 %fusion.10 = f32[256,16,256]{2,0,1:T(8,128)S(1)} fusion(f32[16,256,256]{2,1,0:T(8,128)S(1)} %fusion.3, bf16[1,16,256,256]{3,2,1,0:T(8,128)(2,1)S(1)} %copy-done.2, f32[256,256]{1,0:T(8,128)S(1)} %get-tuple-element.6), kind=kOutput, calls=%fused_computation.15 | convolution fusion | flops 1613758464 | bytes 10747904 | tf_op jit(solution)/shard_map/xpz,ip->xiz/dot_general | solution.py:62
  65.5 1.8 %convert_bitcast_fusion = bf16[1,16,256,256]{3,2,1,0:T(8,128)(2,1)S(1)} fusion(f32[256,16,256]{2,0,1:T(8,128)S(1)} %fusion.10, f32[256,256]{1,0:T(8,128)S(1)} %get-tuple-element.5), kind=kOutput, calls=%fused_computation.14 | convolution fusion | flops 1611661312 | bytes 6553600 | tf_op jit(solution)/shard_map/xyp,ip->xyi/dot_general | solution.py:63
  67.4 1.2 copy.33
  68.6 28.1 %all_to_all.33 = bf16[1,16,256,256]{3,1,0,2:T(8,128)(2,1)S(1)} all-to-all(bf16[1,16,256,256]{3,1,0,2:T(8,128)(2,1)S(1)} %copy.33), channel_id=1, replica_groups=mesh['tile'=8,'view'=4] {'view'}, dimensions={2} | all-to-all | bytes 4194304 | tf_op jit(solution)/shard_map/all_to_all | solution.py:64
  96.6 1.1 fusion.50
  97.7 1.2 fusion.48
  98.9 4.0 %collective-permute-start.2 = (bf16[15,64,256]{2,0,1:T(8,128)(2,1)}, bf16[15,64,256]{2,0,1:T(8,128)(2,1)}, u32[]{:S(2)}, u32[]{:S(2)}) collective-permute-start(bf16[15,64,256]{2,0,1:T(8,128)(2,1)} %get-tuple-element.11), channel_id=1, source_target_pairs={{0,4},{4,8},{8,12},{12,16},{16,20},{20,24},{24,28},{1,5},{5,9},{9,... | collective-permute-start | bytes 1474568 | tf_op jit(solution)/shard_map/ppermute | solution.py:69
  102.9 1.9 %collective-permute-start.3 = (bf16[15,64,256]{2,0,1:T(8,128)(2,1)}, bf16[15,64,256]{2,0,1:T(8,128)(2,1)}, u32[]{:S(2)}, u32[]{:S(2)}) collective-permute-start(bf16[15,64,256]{2,0,1:T(8,128)(2,1)} %get-tuple-element.12), channel_id=1, source_target_pairs={{4,0},{8,4},{12,8},{16,12},{20,16},{24,20},{28,24},{5,1},{9,5},{13... | collective-permute-start | bytes 1474568 | tf_op jit(solution)/shard_map/ppermute | solution.py:70
  105.0 19.8 %collective-permute-done.2 = bf16[15,64,256]{2,0,1:T(8,128)(2,1)} collective-permute-done((bf16[15,64,256]{2,0,1:T(8,128)(2,1)}, bf16[15,64,256]{2,0,1:T(8,128)(2,1)}, u32[]{:S(2)}, u32[]{:S(2)}) %collective-permute-start.2) | collective-permute-done | bytes 491552 | tf_op jit(solution)/shard_map/ppermute | solution.py:69
  124.7 1.2 collective-permute-done.3
  126.0 2.3 %multiply_select_fusion = f32[16,64,256]{2,0,1:T(8,128)S(1)} fusion(f32[46,64,256]{2,0,1:T(8,128)S(1)} %get-tuple-element.22, f32[16,64,256]{2,1,0:T(8,128)} %param.7, bf16[15,64,256]{2,0,1:T(8,128)(2,1)} %collective-permute-done.3, bf16[15,64,256]{2,0,1:T(8,128)(2,1)} %collective-permute-done.2, pred[16,64]{0,1:T(8,128)(4,1)S(1)} %broadcast_bitcast_fusion), kind=kLoop, calls=%fused_computation.23 | loop fusion | flops 1835008 | bytes 4129792 | tf_op jit(solution)/shard_map/jit(_where)/select_n | solution.py:75
  128.3 1.6 %copy.38 = f32[16,64,256]{2,1,0:T(8,128)} copy(f32[16,64,256]{2,0,1:T(8,128)S(1)} %multiply_select_fusion) | data formatting | bytes 2097152 | tf_op jit(solution)/shard_map/jit(_where)/select_n | solution.py:75
  (24 shorter events, 0.7 us)
Async XLA Ops:
  0.0 7.4 %copy-start = (f32[16,3,31]{2,0,1:T(8,128)S(1)}, f32[16,3,31]{2,0,1:T(8,128)}, u32[]{:S(2)}) copy-start(f32[16,3,31]{2,0,1:T(8,128)} %param.8) | copy-start | bytes 17860
  0.0 7.4 %copy-start.1 = (s32[16,3]{0,1:T(4,128)S(1)}, s32[16,3]{0,1:T(4,128)}, u32[]{:S(2)}) copy-start(s32[16,3]{0,1:T(4,128)} %param.9) | copy-start | bytes 580
  0.0 7.6 %copy-start.4 = (s32[4]{0:T(128)S(1)}, s32[4]{0:T(128)}, u32[]{:S(2)}) copy-start(s32[4]{0:T(128)} %param.10) | copy-start | bytes 52
  2.1 25.9 %collective-permute-start = (bf16[15,64,256]{2,0,1:T(8,128)(2,1)S(1)}, bf16[15,64,256]{2,0,1:T(8,128)(2,1)S(1)}, u32[]{:S(2)}, u32[]{:S(2)}) collective-permute-start(bf16[15,64,256]{2,0,1:T(8,128)(2,1)S(1)} %get-tuple-element.13), channel_id=1, source_target_pairs={{0,4},{4,8},{8,12},{12,16},{16,20},{20,24},{24,28},{1,5},{5,9},{9,... | collective-permute-start | bytes 1474568 | tf_op jit(solution)/shard_map/ppermute | solution.py:49
  5.2 22.8 %collective-permute-start.1 = (bf16[15,64,256]{2,0,1:T(8,128)(2,1)S(1)}, bf16[15,64,256]{2,0,1:T(8,128)(2,1)S(1)}, u32[]{:S(2)}, u32[]{:S(2)}) collective-permute-start(bf16[15,64,256]{2,0,1:T(8,128)(2,1)S(1)} %get-tuple-element.14), channel_id=1, source_target_pairs={{4,0},{8,4},{12,8},{16,12},{20,16},{24,20},{28,24},{5,1},{9,5},{13... | collective-permute-start | bytes 1474568 | tf_op jit(solution)/shard_map/ppermute | solution.py:51
  30.6 29.8 %all-to-all-start = ((bf16[4,16,64,256]{3,1,2,0:T(8,128)(2,1)}), bf16[4,16,64,256]{3,1,2,0:T(8,128)(2,1)S(1)}, u32[]{:S(2)}, u32[]{:S(2)}) async-start(bf16[4,16,64,256]{3,1,2,0:T(8,128)(2,1)} %convolution_convert_fusion), calls=%async_computation | async-start | bytes 4194304 | tf_op jit(solution)/shard_map/all_to_all | solution.py:56
  62.2 1.9 %copy-start.2 = (bf16[1,16,256,256]{3,2,1,0:T(8,128)(2,1)S(1)}, bf16[1,16,256,256]{3,2,1,0:T(8,128)(2,1)}, u32[]{:S(2)}) copy-start(bf16[1,16,256,256]{3,2,1,0:T(8,128)(2,1)} %param.6) | copy-start | bytes 6291460
  96.6 8.2 %copy-start.3 = (s32[2,8]{1,0:T(2,128)S(1)}, s32[2,8]{1,0:T(2,128)}, u32[]{:S(2)}) copy-start(s32[2,8]{1,0:T(2,128)} %param.11) | copy-start | bytes 196
  98.9 25.9 %collective-permute-start.2 = (bf16[15,64,256]{2,0,1:T(8,128)(2,1)}, bf16[15,64,256]{2,0,1:T(8,128)(2,1)}, u32[]{:S(2)}, u32[]{:S(2)}) collective-permute-start(bf16[15,64,256]{2,0,1:T(8,128)(2,1)} %get-tuple-element.11), channel_id=1, source_target_pairs={{0,4},{4,8},{8,12},{12,16},{16,20},{20,24},{24,28},{1,5},{5,9},{9,... | collective-permute-start | bytes 1474568 | tf_op jit(solution)/shard_map/ppermute | solution.py:69
  102.9 23.1 %collective-permute-start.3 = (bf16[15,64,256]{2,0,1:T(8,128)(2,1)}, bf16[15,64,256]{2,0,1:T(8,128)(2,1)}, u32[]{:S(2)}, u32[]{:S(2)}) collective-permute-start(bf16[15,64,256]{2,0,1:T(8,128)(2,1)} %get-tuple-element.12), channel_id=1, source_target_pairs={{4,0},{8,4},{12,8},{16,12},{20,16},{24,20},{28,24},{5,1},{9,5},{13... | collective-permute-start | bytes 1474568 | tf_op jit(solution)/shard_map/ppermute | solution.py:70

commit v2 on v1

v2 whole, which is shorter than its diff:
```python
import functools

import jax
import jax.numpy as jnp
from jax import lax
from jax.experimental import pallas as pl
from jax.experimental.pallas import tpu as pltpu
from jax.sharding import PartitionSpec as P

TAPS = 31
HALF = TAPS // 2
GROUP = 8
CHUNK = 16
F32 = jnp.float32
BF16 = jnp.bfloat16
MESH = pl.DeviceIdType.MESH


def dot(a, b):
    return jnp.dot(a, b, preferred_element_type=F32)


def dot_nt(a, b):
    return lax.dot_general(a, b, (((1,), (1,)), ((), ())), preferred_element_type=F32)


def picked_taps(entry, half_ref, psf_ref, taps):
    taps[0:3, 0:TAPS] = psf_ref[entry]
    row = lax.broadcasted_iota(jnp.int32, taps.shape, 0)
    col = lax.broadcasted_iota(jnp.int32, taps.shape, 1)
    width = jnp.where(
        row == 0, half_ref[entry, 0], jnp.where(row == 1, half_ref[entry, 1], half_ref[entry, 2])
    )
    keep = (jnp.abs(col - HALF) <= width) & (col < TAPS) & (row < 3)
    return jnp.where(keep, taps[...], 0.0).astype(BF16).astype(F32)


def band(line, size):
    rolled = pltpu.roll(
        jnp.broadcast_to(line, (size, size)), size - HALF, 1, stride=1, stride_axis=0
    )
    row = lax.broadcasted_iota(jnp.int32, (size, size), 0)
    col = lax.broadcasted_iota(jnp.int32, (size, size), 1)
    return jnp.where(jnp.abs(row - col) <= HALF, rolled, 0.0)


def kernel(
    assign_ref, half_ref, psf_ref, rounded, recorded_hbm, out,
    taps, wide_a, wide_b, cy, cyt, cz, recorded,
    from_low, from_high, mixed, first, second, sent, parts,
    to_low, to_high, back_low, back_high,
    rec_sem, halo_send, halo_recv, mix_send, mix_recv,
    part_send, part_recv, sum_send, sum_recv,
):
    views = parts.shape[0]
    slab, quarter, depth = rounded.shape
    chunks = quarter // CHUNK
    tile, view = lax.axis_index("tile"), lax.axis_index("view")
    last = lax.axis_size("tile") - 1
    has_low, has_high = tile > 0, tile < last

    def ys(c, base=0):
        return pl.ds(pl.multiple_of(base + c * CHUNK, CHUNK), CHUNK)

    def peer(k):
        return lax.rem(view + k, views)

    def remote(src, dst, send, recv, device):
        return pltpu.make_async_remote_copy(
            src_ref=src, dst_ref=dst, send_sem=send, recv_sem=recv,
            device_id=device, device_id_type=MESH,
        )

    def halo_up(c):
        return remote(
            rounded.at[slab - HALF:slab, ys(c)], from_low.at[slab - HALF:slab, ys(c)],
            halo_send.at[0, c], halo_recv.at[0, c], {"tile": tile + 1},
        )

    def halo_down(c):
        return remote(
            rounded.at[0:HALF, ys(c)], from_high.at[0:HALF, ys(c)],
            halo_send.at[1, c], halo_recv.at[1, c], {"tile": tile - 1},
        )

    def mix(k, c):
        return remote(
            mixed.at[peer(k), :, ys(c)], first.at[:, ys(c, view * quarter)],
            mix_send.at[k - 1, c], mix_recv.at[k - 1, c], {"view": peer(k)},
        )

    def part(k, c):
        return remote(
            sent.at[k - 1, :, ys(c)], parts.at[view, :, ys(c)],
            part_send.at[k - 1, c], part_recv.at[k - 1, c], {"view": peer(k)},
        )

    def sum_up(c):
        return remote(
            to_high.at[:, ys(c)], back_low.at[:, ys(c)],
            sum_send.at[0, c], sum_recv.at[0, c], {"tile": tile + 1},
        )

    def sum_down(c):
        return remote(
            to_low.at[:, ys(c)], back_high.at[:, ys(c)],
            sum_send.at[1, c], sum_recv.at[1, c], {"tile": tile - 1},
        )

    def each_chunk(body):
        def step(c, carry):
            body(c)
            return carry
        lax.fori_loop(0, chunks, step, 0)

    rec_copy = pltpu.make_async_copy(recorded_hbm.at[0], recorded, rec_sem)
    rec_copy.start()
    for ref in (from_low, from_high, back_low, back_high):
        ref[...] = jnp.zeros_like(ref)
    barrier = pltpu.get_barrier_semaphore()
    for k in range(1, views):
        pl.semaphore_signal(barrier, inc=1, device_id={"view": peer(k)}, device_id_type=MESH)

    @pl.when(has_low)
    def _():
        pl.semaphore_signal(barrier, inc=1, device_id={"tile": tile - 1}, device_id_type=MESH)

    @pl.when(has_high)
    def _():
        pl.semaphore_signal(barrier, inc=1, device_id={"tile": tile + 1}, device_id_type=MESH)

    pl.semaphore_wait(
        barrier, views - 1 + has_low.astype(jnp.int32) + has_high.astype(jnp.int32)
    )

    def start_halo(c):
        @pl.when(has_high)
        def _():
            halo_up(c).start()

        @pl.when(has_low)
        def _():
            halo_down(c).start()

    each_chunk(start_halo)

    taps[...] = jnp.zeros_like(taps)
    rows, cols = slab * GROUP, 3 * slab * GROUP
    tap = lax.broadcasted_iota(jnp.int32, (taps.shape[1], cols), 0)
    spot = lax.broadcasted_iota(jnp.int32, (taps.shape[1], cols), 1)
    spread = ((spot == GROUP * (tap + slab - HALF)) & (tap < TAPS)).astype(F32).astype(BF16)
    for s in range(views):
        lines = picked_taps(assign_ref[s], half_ref, psf_ref, taps)
        line = dot(lines.astype(BF16), spread)[0:1]
        block = pltpu.roll(jnp.broadcast_to(line, (rows, cols)), 0, 1, stride=1, stride_axis=0)
        wide_a[s * rows:(s + 1) * rows, :] = block.astype(BF16)
        wide_b[:, s * rows:(s + 1) * rows] = block.T.astype(BF16)
    lines = picked_taps(assign_ref[view], half_ref, psf_ref, taps)
    totals = jnp.sum(lines, axis=1, keepdims=True)
    scale = 1.0 / (totals[0:1] * totals[1:2] * totals[2:3])
    across = band(lines[1:2], cy.shape[0])
    cy[...] = across.astype(BF16)
    cyt[...] = across.T.astype(BF16)
    cz[...] = band(lines[2:3], depth).astype(BF16)

    def blur_first(c):
        @pl.when(has_low)
        def _():
            halo_up(c).wait_recv()

        @pl.when(has_high)
        def _():
            halo_down(c).wait_recv()

        cells = jnp.concatenate(
            [from_low[:, ys(c), :], rounded[:, ys(c), :], from_high[:, ys(c), :]], axis=0
        ).astype(F32)
        halves = []
        for h in range(0, CHUNK, GROUP):
            some = cells[:, h:h + GROUP, :].reshape(cols, depth).astype(BF16)
            halves.append(dot(wide_a[...], some).reshape(views * slab, GROUP, depth))
        mixed[:, :, ys(c), :] = (
            jnp.concatenate(halves, axis=1).astype(BF16).reshape(views, slab, CHUNK, depth)
        )
        for k in range(1, views):
            mix(k, c).start()
        first[:, ys(c, view * quarter), :] = mixed[view, :, ys(c), :]

    each_chunk(blur_first)

    def wait_mix(c):
        for k in range(1, views):
            mix(k, c).wait_recv()

    each_chunk(wait_mix)
    rec_copy.wait()

    def plane(i, carry):
        blurred = dot(cy[...], first[i]).astype(BF16)
        blurred = dot_nt(blurred, cz[...]) * scale
        ratio = (recorded[i].astype(F32) / blurred).astype(BF16)
        second[i] = dot(cyt[...], ratio).astype(BF16)
        return carry

    lax.fori_loop(0, slab, plane, 0)

    def spread_parts(c):
        for k in list(range(1, views)) + [0]:
            lines = second[:, ys(c, peer(k) * quarter), :].reshape(slab * CHUNK, depth)
            value = (dot(lines, cz[...]) * scale).astype(BF16).reshape(slab, CHUNK, depth)
            if k:
                sent[k - 1, :, ys(c), :] = value
                part(k, c).start()
            else:
                parts[view, :, ys(c), :] = value

    each_chunk(spread_parts)

    def blur_last(c):
        for k in range(1, views):
            part(k, c).wait_recv()
        cells = parts[:, :, ys(c), :].astype(F32).reshape(views * slab, CHUNK, depth)
        halves = []
        for h in range(0, CHUNK, GROUP):
            some = cells[:, h:h + GROUP, :].reshape(views * rows, depth).astype(BF16)
            halves.append(dot(wide_b[...], some).reshape(3 * slab, GROUP, depth))
        wide = jnp.concatenate(halves, axis=1)
        out[:, ys(c), :] = wide[slab:2 * slab]
        for block, target, spare in (
            (wide[:slab], to_low, 0), (wide[2 * slab:], to_high, slab - 1)
        ):
            mean = (jnp.sum(block, axis=1) * (1.0 / CHUNK)).astype(BF16)
            target[:, ys(c), :] = (block - mean.astype(F32)[:, None, :]).astype(BF16)
            target[spare, ys(c), :] = mean

        @pl.when(has_high)
        def _():
            sum_up(c).start()

        @pl.when(has_low)
        def _():
            sum_down(c).start()

    each_chunk(blur_last)

    def add_sums(c):
        @pl.when(has_low)
        def _():
            sum_up(c).wait_recv()

        @pl.when(has_high)
        def _():
            sum_down(c).wait_recv()

        for came, spare in ((back_low, slab - 1), (back_high, 0)):
            mean = came[spare, ys(c), :].astype(F32)[:, None, :]
            added = came[:, ys(c), :].astype(F32) + mean
            for i in range(slab):
                if i != spare:
                    out[i, ys(c), :] += added[i]

    each_chunk(add_sums)

    def wait_sends(c):
        for k in range(1, views):
            mix(k, c).wait_send()
            part(k, c).wait_send()

        @pl.when(has_high)
        def _():
            halo_up(c).wait_send()
            sum_up(c).wait_send()

        @pl.when(has_low)
        def _():
            halo_down(c).wait_send()
            sum_down(c).wait_send()

    each_chunk(wait_sends)


def shards(recorded, estimate, psf_taps, half_width, assign, flags):
    views = lax.axis_size("view")
    slab, quarter, depth = estimate.shape
    full_y = recorded.shape[2]
    chunks = quarter // CHUNK
    rows, cols = slab * GROUP, 3 * slab * GROUP
    cells = jnp.repeat(jnp.repeat(flags, 8, axis=0), 8, axis=1)[:, :, None] > 0
    vmem = pl.BlockSpec(memory_space=pltpu.VMEM)
    smem = pl.BlockSpec(memory_space=pltpu.SMEM)
    dma = pltpu.SemaphoreType.DMA
    edge = pltpu.VMEM((slab, quarter, depth), BF16)
    whole = pltpu.VMEM((slab, full_y, depth), BF16)
    total = pl.pallas_call(
        kernel,
        out_shape=jax.ShapeDtypeStruct(estimate.shape, F32),
        in_specs=[smem, smem, vmem, vmem, pl.BlockSpec(memory_space=pl.ANY)],
        out_specs=vmem,
        scratch_shapes=[
            pltpu.VMEM((8, 256), F32),
            pltpu.VMEM((views * rows, cols), BF16),
            pltpu.VMEM((cols, views * rows), BF16),
            pltpu.VMEM((full_y, full_y), BF16),
            pltpu.VMEM((full_y, full_y), BF16),
            pltpu.VMEM((depth, depth), BF16),
            whole,
            edge, edge,
            pltpu.VMEM((views, slab, quarter, depth), BF16),
            whole, whole,
            pltpu.VMEM((views - 1, slab, quarter, depth), BF16),
            pltpu.VMEM((views, slab, quarter, depth), BF16),
            edge, edge, edge, edge,
            dma,
            dma((2, chunks)), dma((2, chunks)),
            dma((views - 1, chunks)), dma((views - 1, chunks)),
            dma((views - 1, chunks)), dma((views - 1, chunks)),
            dma((2, chunks)), dma((2, chunks)),
        ],
        compiler_params=pltpu.CompilerParams(collective_id=0, has_side_effects=True),
        name="deconvolve",
    )(assign, half_width, psf_taps, estimate.astype(BF16), recorded)
    return jnp.where(cells, estimate * (total / views), estimate)


def solution(mesh):
    placed = (
        P("view", "tile", None, None),
        P("tile", "view", None),
        P(),
        P(),
        P(),
        P("tile", "view"),
    )
    return jax.shard_map(
        shards, mesh=mesh, in_specs=placed, out_specs=P("tile", "view", None), check_vma=False
    )
```

time: 132 us -> 90.7 us (0.69); the launches traced: 130 us -> 90.5 us
  Pallas kernels: 0 us -> 82.9 us
  waiting for transfers between devices: 64.1 us -> 0 us
  blocking collectives: 28.1 us -> 0 us
  starting transfers between devices: 16.3 us -> 0 us
  matrix products: 10.9 us -> 0 us
  local copies, waits for them, and re-layouts: 6.14 us -> 3 us
    pallas_call x0 -> x1, Pallas kernels: none -> 82.9 us  [shards(): pl.pallas_call(kernel, out_shape=jax.ShapeDtypeStruct(estimate.shape, F32...]
    ppermute x4 -> x0, waiting for transfers between devices: 41 us -> none  [the longest x1 20 us: shards(): lax.ppermute(rounded[slab - HALF:], 'tile', up)]
    all_to_all x1 -> x0, blocking collectives: 28.1 us -> none  [shards(): lax.all_to_all(back.astype(jnp.bfloat16)[None], 'view', split_axis=2, con...]
    all_to_all x1 -> x0, waiting for transfers between devices: 23.1 us -> none  [shards(): lax.all_to_all(stacked.astype(jnp.bfloat16), 'view', split_axis=0, concat...]
    ppermute x4 -> x0, starting transfers between devices: 11.2 us -> none  [the longest x1 4.03 us: shards(): below = lax.ppermute(spread[slab + HALF:], 'tile', up).astype(jnp.float32)]
    dot_general x8 -> x0, matrix products: 10.9 us -> none  [the longest x1 2.59 us: shards(): stacked = jnp.einsum('pyz,spi->siyz', padded, first_all, precision=HIGH)]
    all_to_all x1 -> x0, starting transfers between devices: 5.11 us -> none  [shards(): lax.all_to_all(stacked.astype(jnp.bfloat16), 'view', split_axis=0, concat...]
    convert_element_type x0 -> x1, other arithmetic: none -> 2.08 us  [shards(): estimate.astype(BF16)]
  transfers between devices with their start and end apart: 5 -> 0, of which waited for: 4 -> 0; matrix products, arithmetic and copies ran while one was open for 2% -> 0% of each run, Pallas kernels for 0% -> 0%
where the time goes in v2:
time: 90.7 us; the launch traced here: 90.5 us
  Pallas kernels  82.9 us (91%)
  other arithmetic  4.5 us (5%)
  local copies, waits for them, and re-layouts  3 us (3%)
    pallas_call x1, Pallas kernels, shards(): pl.pallas_call(kernel, out_shape=jax.ShapeDtypeStruct(estimate.shape, F32...  82.9 us
    unnamed x6, local copies, waits for them, and re-layouts  2.82 us
    select_n x1, other arithmetic, shards(): return jnp.where(cells, estimate * (total / views), estimate)  2.41 us
    convert_element_type x1, other arithmetic, shards(): estimate.astype(BF16)  2.08 us

profile of v2, /device:TPU:21, one launch (start us, length us, event | category | flops | bytes accessed | tf_op | source)
XLA Modules:
  0.0 90.5 jit_solution(5523793439056377673)
XLA Ops:
  0.0 2.1 %convert_element_type.3.rounded = bf16[16,64,256]{2,1,0:T(8,128)(2,1)} convert(f32[16,64,256]{2,1,0:T(8,128)} %param.7) | non-fusion elementwise | flops 262144 | bytes 1572864 | tf_op jit(solution)/shard_map/convert_element_type | solution.py:321
  2.1 0.0 copy-start.1
  2.1 0.0 copy-start
  2.1 1.4 %copy.12.psf_ref = f32[16,3,31]{2,1,0:T(4,128)} copy(f32[16,3,31]{2,0,1:T(8,128)} %param.8) | data formatting | bytes 11904 | tf_op args[2]
  3.5 1.4 %copy.11.half_ref = s32[16,3]{1,0:T(8,128)} copy(s32[16,3]{0,1:T(4,128)} %param.9) | data formatting | bytes 384 | tf_op args[3]
  4.9 82.9 %deconvolve.1 = f32[16,64,256]{2,1,0:T(8,128)} custom-call(s32[4]{0:T(128)} %assign_ref.1, s32[16,3]{1,0:T(8,128)} %copy.11.half_ref, f32[16,3,31]{2,1,0:T(4,128)} %copy.12.psf_ref, bf16[16,64,256]{2,1,0:T(8,128)(2,1)} %convert_element_type.3.rounded, bf16[1,16,256,256]{3,2,1,0:T(8,128)(2,1)} %recorded_hbm.1), custom_call_target="tpu_custom_call" | custom-call | tf_op jit(solution)/shard_map/deconvolve/pallas_call | solution.py:294
  87.9 0.0 copy-done.1
  87.9 0.1 copy.9
  88.0 0.1 copy.10
  88.1 0.0 copy-done
  88.1 2.4 %multiply_select_fusion = f32[16,64,256]{2,1,0:T(8,128)} fusion(f32[16,64,256]{2,1,0:T(8,128)S(1)} %copy-done, f32[16,64,256]{2,1,0:T(8,128)} %deconvolve.1, pred[16,64]{1,0:T(8,128)(4,1)S(1)} %copy.10), kind=kLoop, calls=%fused_computation | loop fusion | flops 786432 | bytes 3146752 | tf_op jit(solution)/shard_map/jit(_where)/select_n | solution.py:322
  (3 shorter events, 0.0 us)
Async XLA Ops:
  2.1 85.8 %copy-start.1 = (s32[2,8]{1,0:T(2,128)S(1)}, s32[2,8]{1,0:T(2,128)}, u32[]{:S(2)}) copy-start(s32[2,8]{1,0:T(2,128)} %param.11) | copy-start | bytes 196
  2.1 86.0 %copy-start = (f32[16,64,256]{2,1,0:T(8,128)S(1)}, f32[16,64,256]{2,1,0:T(8,128)}, u32[]{:S(2)}) copy-start(f32[16,64,256]{2,1,0:T(8,128)} %param.7) | copy-start | bytes 3145732

commit v3 on v2

--- a/solution.py
+++ b/solution.py
@@ -1,5 +1,3 @@
-import functools
-
 import jax
 import jax.numpy as jnp
 from jax import lax
@@ -11,6 +9,7 @@
 HALF = TAPS // 2
 GROUP = 8
 CHUNK = 16
+PLANES = 4
 F32 = jnp.float32
 BF16 = jnp.bfloat16
 MESH = pl.DeviceIdType.MESH
@@ -25,11 +24,12 @@
 
 
 def picked_taps(entry, half_ref, psf_ref, taps):
-    taps[0:3, 0:TAPS] = psf_ref[entry]
+    for d in range(3):
+        taps[d:d + 1, 0:TAPS] = psf_ref[d, pl.ds(entry, 1), :]
     row = lax.broadcasted_iota(jnp.int32, taps.shape, 0)
     col = lax.broadcasted_iota(jnp.int32, taps.shape, 1)
     width = jnp.where(
-        row == 0, half_ref[entry, 0], jnp.where(row == 1, half_ref[entry, 1], half_ref[entry, 2])
+        row == 0, half_ref[0, entry], jnp.where(row == 1, half_ref[1, entry], half_ref[2, entry])
     )
     keep = (jnp.abs(col - HALF) <= width) & (col < TAPS) & (row < 3)
     return jnp.where(keep, taps[...], 0.0).astype(BF16).astype(F32)
@@ -47,10 +47,10 @@
 def kernel(
     assign_ref, half_ref, psf_ref, rounded, recorded_hbm, out,
     taps, wide_a, wide_b, cy, cyt, cz, recorded,
-    from_low, from_high, mixed, first, second, sent, parts,
+    from_low, from_high, mixed, first, second, parts,
     to_low, to_high, back_low, back_high,
     rec_sem, halo_send, halo_recv, mix_send, mix_recv,
-    part_send, part_recv, sum_send, sum_recv,
+    part_send, part_recv, early_send, early_recv, sum_send, sum_recv,
 ):
     views = parts.shape[0]
     slab, quarter, depth = rounded.shape
@@ -91,9 +91,18 @@
 
     def part(k, c):
         return remote(
-            sent.at[k - 1, :, ys(c)], parts.at[view, :, ys(c)],
+            second.at[:, ys(c, peer(k) * quarter)], parts.at[view, :, ys(c)],
             part_send.at[k - 1, c], part_recv.at[k - 1, c], {"view": peer(k)},
         )
+
+    def early(k, g):
+        some = pl.ds(g * PLANES, PLANES)
+        return remote(
+            second.at[some, ys(0, peer(k) * quarter)], parts.at[view, some, ys(0)],
+            early_send.at[k - 1, g], early_recv.at[k - 1, g], {"view": peer(k)},
+        )
+
+    groups = slab // PLANES
 
     def sum_up(c):
         return remote(
@@ -142,7 +151,7 @@
         def _():
             halo_down(c).start()
 
-    each_chunk(start_halo)
+    start_halo(0)
 
     taps[...] = jnp.zeros_like(taps)
     rows, cols = slab * GROUP, 3 * slab * GROUP
@@ -172,6 +181,10 @@
         def _():
             halo_down(c).wait_recv()
 
+        @pl.when(c + 1 < chunks)
+        def _():
+            start_halo(c + 1)
+
         cells = jnp.concatenate(
             [from_low[:, ys(c), :], rounded[:, ys(c), :], from_high[:, ys(c), :]], axis=0
         ).astype(F32)
@@ -195,30 +208,45 @@
     each_chunk(wait_mix)
     rec_copy.wait()
 
-    def plane(i, carry):
+    def plane(i):
         blurred = dot(cy[...], first[i]).astype(BF16)
         blurred = dot_nt(blurred, cz[...]) * scale
         ratio = (recorded[i].astype(F32) / blurred).astype(BF16)
-        second[i] = dot(cyt[...], ratio).astype(BF16)
+        back = dot(cyt[...], ratio).astype(BF16)
+        second[i] = (dot(back, cz[...]) * scale).astype(BF16)
+
+    def plane_group(g, carry):
+        for i in range(PLANES):
+            plane(g * PLANES + i)
+        for k in range(1, views):
+            early(k, g).start()
         return carry
 
-    lax.fori_loop(0, slab, plane, 0)
-
-    def spread_parts(c):
-        for k in list(range(1, views)) + [0]:
-            lines = second[:, ys(c, peer(k) * quarter), :].reshape(slab * CHUNK, depth)
-            value = (dot(lines, cz[...]) * scale).astype(BF16).reshape(slab, CHUNK, depth)
-            if k:
-                sent[k - 1, :, ys(c), :] = value
-                part(k, c).start()
-            else:
-                parts[view, :, ys(c), :] = value
-
-    each_chunk(spread_parts)
+    lax.fori_loop(0, groups, plane_group, 0)
+
+    def start_parts(c, carry):
+        for k in range(1, views):
+            part(k, c).start()
+        return carry
+
+    lax.fori_loop(1, chunks, start_parts, 0)
+
+    def wait_early(g, carry):
+        for k in range(1, views):
+            early(k, g).wait_recv()
+        return carry
 
     def blur_last(c):
-        for k in range(1, views):
-            part(k, c).wait_recv()
+        @pl.when(c == 0)
+        def _():
+            lax.fori_loop(0, groups, wait_early, 0)
+
+        @pl.when(c > 0)
+        def _():
+            for k in range(1, views):
+                part(k, c).wait_recv()
+
+        parts[view, :, ys(c), :] = second[:, ys(c, view * quarter), :]
         cells = parts[:, :, ys(c), :].astype(F32).reshape(views * slab, CHUNK, depth)
         halves = []
         for h in range(0, CHUNK, GROUP):
@@ -264,7 +292,11 @@
     def wait_sends(c):
         for k in range(1, views):
             mix(k, c).wait_send()
-            part(k, c).wait_send()
+
+        @pl.when(c > 0)
+        def _():
+            for k in range(1, views):
+                part(k, c).wait_send()
 
         @pl.when(has_high)
         def _():
@@ -277,6 +309,13 @@
             sum_down(c).wait_send()
 
     each_chunk(wait_sends)
+
+    def wait_early_sends(g, carry):
+        for k in range(1, views):
+            early(k, g).wait_send()
+        return carry
+
+    lax.fori_loop(0, groups, wait_early_sends, 0)
 
 
 def shards(recorded, estimate, psf_taps, half_width, assign, flags):
@@ -307,18 +346,18 @@
             edge, edge,
             pltpu.VMEM((views, slab, quarter, depth), BF16),
             whole, whole,
-            pltpu.VMEM((views - 1, slab, quarter, depth), BF16),
             pltpu.VMEM((views, slab, quarter, depth), BF16),
             edge, edge, edge, edge,
             dma,
             dma((2, chunks)), dma((2, chunks)),
             dma((views - 1, chunks)), dma((views - 1, chunks)),
             dma((views - 1, chunks)), dma((views - 1, chunks)),
+            dma((views - 1, slab // PLANES)), dma((views - 1, slab // PLANES)),
             dma((2, chunks)), dma((2, chunks)),
         ],
         compiler_params=pltpu.CompilerParams(collective_id=0, has_side_effects=True),
         name="deconvolve",
-    )(assign, half_width, psf_taps, estimate.astype(BF16), recorded)
+    )(assign, half_width.T, psf_taps.transpose(1, 0, 2), estimate.astype(BF16), recorded)
     return jnp.where(cells, estimate * (total / views), estimate)
 
 

time: 90.7 us -> 79.2 us (0.87)
  Pallas kernels: 82.9 us -> 74.3 us
  local copies, waits for them, and re-layouts: 3 us -> 0.19 us
    pallas_call x1, Pallas kernels: 82.9 us -> 74.3 us  [shards(): pl.pallas_call(kernel, out_shape=jax.ShapeDtypeStruct(estimate.shape, F32...]
    unnamed x6 -> x4, local copies, waits for them, and re-layouts: 2.82 us -> 0.01 us
where the time goes in v3:
time: 79.2 us; the launch traced here: 79 us
  Pallas kernels  74.3 us (94%)
  other arithmetic  4.5 us (6%)
    pallas_call x1, Pallas kernels, shards(): pl.pallas_call(kernel, out_shape=jax.ShapeDtypeStruct(estimate.shape, F32...  74.3 us
    select_n x1, other arithmetic, shards(): return jnp.where(cells, estimate * (total / views), estimate)  2.41 us
    convert_element_type x1, other arithmetic, shards(): estimate.astype(BF16)  2.08 us

profile of v3, /device:TPU:21, one launch (start us, length us, event | category | flops | bytes accessed | tf_op | source)
XLA Modules:
  0.0 79.0 jit_solution(5683488187429701575)
XLA Ops:
  0.0 2.1 %convert_element_type.3.rounded = bf16[16,64,256]{2,1,0:T(8,128)(2,1)} convert(f32[16,64,256]{2,1,0:T(8,128)} %param.7) | non-fusion elementwise | flops 262144 | bytes 1572864 | tf_op jit(solution)/shard_map/convert_element_type | solution.py:360
  2.1 0.0 copy-start.1
  2.1 0.0 copy-start
  2.1 74.3 %deconvolve.1 = f32[16,64,256]{2,1,0:T(8,128)} custom-call(s32[4]{0:T(128)} %assign_ref.1, s32[3,16]{1,0:T(4,128)} %bitcast.7, f32[3,16,31]{2,1,0:T(8,128)} %bitcast.6, bf16[16,64,256]{2,1,0:T(8,128)(2,1)} %convert_element_type.3.rounded, bf16[1,16,256,256]{3,2,1,0:T(8,128)(2,1)} %recorded_hbm.1), custom_call_target="tpu_custom_call" | custom-call | tf_op jit(solution)/shard_map/deconvolve/pallas_call | solution.py:333
  76.4 0.0 copy-done.1
  76.4 0.1 copy.7
  76.5 0.1 copy.8
  76.6 0.0 copy-done
  76.6 2.4 %multiply_select_fusion = f32[16,64,256]{2,1,0:T(8,128)} fusion(f32[16,64,256]{2,1,0:T(8,128)S(1)} %copy-done, f32[16,64,256]{2,1,0:T(8,128)} %deconvolve.1, pred[16,64]{1,0:T(8,128)(4,1)S(1)} %copy.8), kind=kLoop, calls=%fused_computation | loop fusion | flops 786432 | bytes 3146752 | tf_op jit(solution)/shard_map/jit(_where)/select_n | solution.py:361
  (3 shorter events, 0.0 us)
Async XLA Ops:
  2.1 74.3 %copy-start.1 = (s32[2,8]{1,0:T(2,128)S(1)}, s32[2,8]{1,0:T(2,128)}, u32[]{:S(2)}) copy-start(s32[2,8]{1,0:T(2,128)} %param.11) | copy-start | bytes 196
  2.1 74.5 %copy-start = (f32[16,64,256]{2,1,0:T(8,128)S(1)}, f32[16,64,256]{2,1,0:T(8,128)}, u32[]{:S(2)}) copy-start(f32[16,64,256]{2,1,0:T(8,128)} %param.7) | copy-start | bytes 3145732

commit v4 on v3

--- a/solution.py
+++ b/solution.py
@@ -10,6 +10,8 @@
 GROUP = 8
 CHUNK = 16
 PLANES = 4
+LANES = 128
+STAGGER = 1
 F32 = jnp.float32
 BF16 = jnp.bfloat16
 MESH = pl.DeviceIdType.MESH
@@ -45,8 +47,8 @@
 
 
 def kernel(
-    assign_ref, half_ref, psf_ref, rounded, recorded_hbm, out,
-    taps, wide_a, wide_b, cy, cyt, cz, recorded,
+    assign_ref, half_ref, psf_ref, estimate, recorded_hbm, out,
+    rounded, taps, wide_a, wide_b, cy, cyt, cz, recorded,
     from_low, from_high, mixed, first, second, parts,
     to_low, to_high, back_low, back_high,
     rec_sem, halo_send, halo_recv, mix_send, mix_recv,
@@ -54,13 +56,17 @@
 ):
     views = parts.shape[0]
     slab, quarter, depth = rounded.shape
-    chunks = quarter // CHUNK
+    halves = depth // LANES
+    pieces = (quarter // CHUNK) * halves
     tile, view = lax.axis_index("tile"), lax.axis_index("view")
     last = lax.axis_size("tile") - 1
     has_low, has_high = tile > 0, tile < last
 
     def ys(c, base=0):
-        return pl.ds(pl.multiple_of(base + c * CHUNK, CHUNK), CHUNK)
+        return pl.ds(pl.multiple_of(base + lax.div(c, halves) * CHUNK, CHUNK), CHUNK)
+
+    def zs(c):
+        return pl.ds(pl.multiple_of(lax.rem(c, halves) * LANES, LANES), LANES)
 
     def peer(k):
         return lax.rem(view + k, views)
@@ -73,25 +79,25 @@
 
     def halo_up(c):
         return remote(
-            rounded.at[slab - HALF:slab, ys(c)], from_low.at[slab - HALF:slab, ys(c)],
+            rounded.at[slab - HALF:slab, ys(c), zs(c)], from_low.at[slab - HALF:slab, ys(c), zs(c)],
             halo_send.at[0, c], halo_recv.at[0, c], {"tile": tile + 1},
         )
 
     def halo_down(c):
         return remote(
-            rounded.at[0:HALF, ys(c)], from_high.at[0:HALF, ys(c)],
+            rounded.at[0:HALF, ys(c), zs(c)], from_high.at[0:HALF, ys(c), zs(c)],
             halo_send.at[1, c], halo_recv.at[1, c], {"tile": tile - 1},
         )
 
     def mix(k, c):
         return remote(
-            mixed.at[peer(k), :, ys(c)], first.at[:, ys(c, view * quarter)],
+            mixed.at[peer(k), :, ys(c), zs(c)], first.at[:, ys(c, view * quarter), zs(c)],
             mix_send.at[k - 1, c], mix_recv.at[k - 1, c], {"view": peer(k)},
         )
 
     def part(k, c):
         return remote(
-            second.at[:, ys(c, peer(k) * quarter)], parts.at[view, :, ys(c)],
+            second.at[:, ys(c, peer(k) * quarter), zs(c)], parts.at[view, :, ys(c), zs(c)],
             part_send.at[k - 1, c], part_recv.at[k - 1, c], {"view": peer(k)},
         )
 
@@ -106,13 +112,13 @@
 
     def sum_up(c):
         return remote(
-            to_high.at[:, ys(c)], back_low.at[:, ys(c)],
+            to_high.at[:, ys(c), zs(c)], back_low.at[:, ys(c), zs(c)],
             sum_send.at[0, c], sum_recv.at[0, c], {"tile": tile + 1},
         )
 
     def sum_down(c):
         return remote(
-            to_low.at[:, ys(c)], back_high.at[:, ys(c)],
+            to_low.at[:, ys(c), zs(c)], back_high.at[:, ys(c), zs(c)],
             sum_send.at[1, c], sum_recv.at[1, c], {"tile": tile - 1},
         )
 
@@ -120,10 +126,11 @@
         def step(c, carry):
             body(c)
             return carry
-        lax.fori_loop(0, chunks, step, 0)
+        lax.fori_loop(0, pieces, step, 0)
 
     rec_copy = pltpu.make_async_copy(recorded_hbm.at[0], recorded, rec_sem)
     rec_copy.start()
+    rounded[...] = estimate[...].astype(BF16)
     for ref in (from_low, from_high, back_low, back_high):
         ref[...] = jnp.zeros_like(ref)
     barrier = pltpu.get_barrier_semaphore()
@@ -164,6 +171,8 @@
         block = pltpu.roll(jnp.broadcast_to(line, (rows, cols)), 0, 1, stride=1, stride_axis=0)
         wide_a[s * rows:(s + 1) * rows, :] = block.astype(BF16)
         wide_b[:, s * rows:(s + 1) * rows] = block.T.astype(BF16)
+        if s == STAGGER:
+            start_halo(1)
     lines = picked_taps(assign_ref[view], half_ref, psf_ref, taps)
     totals = jnp.sum(lines, axis=1, keepdims=True)
     scale = 1.0 / (totals[0:1] * totals[1:2] * totals[2:3])
@@ -181,23 +190,23 @@
         def _():
             halo_down(c).wait_recv()
 
-        @pl.when(c + 1 < chunks)
-        def _():
-            start_halo(c + 1)
+        @pl.when(c + 2 < pieces)
+        def _():
+            start_halo(c + 2)
 
         cells = jnp.concatenate(
-            [from_low[:, ys(c), :], rounded[:, ys(c), :], from_high[:, ys(c), :]], axis=0
+            [from_low[:, ys(c), zs(c)], rounded[:, ys(c), zs(c)], from_high[:, ys(c), zs(c)]], axis=0
         ).astype(F32)
-        halves = []
+        blurs = []
         for h in range(0, CHUNK, GROUP):
-            some = cells[:, h:h + GROUP, :].reshape(cols, depth).astype(BF16)
-            halves.append(dot(wide_a[...], some).reshape(views * slab, GROUP, depth))
-        mixed[:, :, ys(c), :] = (
-            jnp.concatenate(halves, axis=1).astype(BF16).reshape(views, slab, CHUNK, depth)
+            some = cells[:, h:h + GROUP, :].reshape(cols, LANES).astype(BF16)
+            blurs.append(dot(wide_a[...], some).reshape(views * slab, GROUP, LANES))
+        mixed[:, :, ys(c), zs(c)] = (
+            jnp.concatenate(blurs, axis=1).astype(BF16).reshape(views, slab, CHUNK, LANES)
         )
         for k in range(1, views):
             mix(k, c).start()
-        first[:, ys(c, view * quarter), :] = mixed[view, :, ys(c), :]
+        first[:, ys(c, view * quarter), zs(c)] = mixed[view, :, ys(c), zs(c)]
 
     each_chunk(blur_first)
 
@@ -229,7 +238,7 @@
             part(k, c).start()
         return carry
 
-    lax.fori_loop(1, chunks, start_parts, 0)
+    lax.fori_loop(halves, pieces, start_parts, 0)
 
     def wait_early(g, carry):
         for k in range(1, views):
@@ -241,25 +250,25 @@
         def _():
             lax.fori_loop(0, groups, wait_early, 0)
 
-        @pl.when(c > 0)
+        @pl.when(c >= halves)
         def _():
             for k in range(1, views):
                 part(k, c).wait_recv()
 
-        parts[view, :, ys(c), :] = second[:, ys(c, view * quarter), :]
-        cells = parts[:, :, ys(c), :].astype(F32).reshape(views * slab, CHUNK, depth)
-        halves = []
+        parts[view, :, ys(c), zs(c)] = second[:, ys(c, view * quarter), zs(c)]
+        cells = parts[:, :, ys(c), zs(c)].astype(F32).reshape(views * slab, CHUNK, LANES)
+        blurs = []
         for h in range(0, CHUNK, GROUP):
-            some = cells[:, h:h + GROUP, :].reshape(views * rows, depth).astype(BF16)
-            halves.append(dot(wide_b[...], some).reshape(3 * slab, GROUP, depth))
-        wide = jnp.concatenate(halves, axis=1)
-        out[:, ys(c), :] = wide[slab:2 * slab]
+            some = cells[:, h:h + GROUP, :].reshape(views * rows, LANES).astype(BF16)
+            blurs.append(dot(wide_b[...], some).reshape(3 * slab, GROUP, LANES))
+        wide = jnp.concatenate(blurs, axis=1)
+        out[:, ys(c), zs(c)] = wide[slab:2 * slab]
         for block, target, spare in (
             (wide[:slab], to_low, 0), (wide[2 * slab:], to_high, slab - 1)
         ):
             mean = (jnp.sum(block, axis=1) * (1.0 / CHUNK)).astype(BF16)
-            target[:, ys(c), :] = (block - mean.astype(F32)[:, None, :]).astype(BF16)
-            target[spare, ys(c), :] = mean
+            target[:, ys(c), zs(c)] = (block - mean.astype(F32)[:, None, :]).astype(BF16)
+            target[spare, ys(c), zs(c)] = mean
 
         @pl.when(has_high)
         def _():
@@ -281,11 +290,11 @@
             sum_down(c).wait_recv()
 
         for came, spare in ((back_low, slab - 1), (back_high, 0)):
-            mean = came[spare, ys(c), :].astype(F32)[:, None, :]
-            added = came[:, ys(c), :].astype(F32) + mean
+            mean = came[spare, ys(c), zs(c)].astype(F32)[:, None, :]
+            added = came[:, ys(c), zs(c)].astype(F32) + mean
             for i in range(slab):
                 if i != spare:
-                    out[i, ys(c), :] += added[i]
+                    out[i, ys(c), zs(c)] += added[i]
 
     each_chunk(add_sums)
 
@@ -293,7 +302,7 @@
         for k in range(1, views):
             mix(k, c).wait_send()
 
-        @pl.when(c > 0)
+        @pl.when(c >= halves)
         def _():
             for k in range(1, views):
                 part(k, c).wait_send()
@@ -322,7 +331,7 @@
     views = lax.axis_size("view")
     slab, quarter, depth = estimate.shape
     full_y = recorded.shape[2]
-    chunks = quarter // CHUNK
+    chunks = (quarter // CHUNK) * (depth // LANES)
     rows, cols = slab * GROUP, 3 * slab * GROUP
     cells = jnp.repeat(jnp.repeat(flags, 8, axis=0), 8, axis=1)[:, :, None] > 0
     vmem = pl.BlockSpec(memory_space=pltpu.VMEM)
@@ -336,6 +345,7 @@
         in_specs=[smem, smem, vmem, vmem, pl.BlockSpec(memory_space=pl.ANY)],
         out_specs=vmem,
         scratch_shapes=[
+            edge,
             pltpu.VMEM((8, 256), F32),
             pltpu.VMEM((views * rows, cols), BF16),
             pltpu.VMEM((cols, views * rows), BF16),
@@ -357,7 +367,7 @@
         ],
         compiler_params=pltpu.CompilerParams(collective_id=0, has_side_effects=True),
         name="deconvolve",
-    )(assign, half_width.T, psf_taps.transpose(1, 0, 2), estimate.astype(BF16), recorded)
+    )(assign, half_width.T, psf_taps.transpose(1, 0, 2), estimate, recorded)
     return jnp.where(cells, estimate * (total / views), estimate)
 
 

time: 79.2 us -> 76.5 us (0.966)
  Pallas kernels: 74.3 us -> 72.5 us
  other arithmetic: 4.5 us -> 3.08 us
    convert_element_type x1 -> x0, other arithmetic: 2.08 us -> none  [shards(): estimate.astype(BF16)]
    pallas_call x1, Pallas kernels: 74.3 us -> 72.5 us  [shards(): pl.pallas_call(kernel, out_shape=jax.ShapeDtypeStruct(estimate.shape, F32...]
where the time goes in v4:
time: 76.5 us; the launch traced here: 75.8 us
  Pallas kernels  72.5 us (95%)
  other arithmetic  3.08 us (4%)
    pallas_call x1, Pallas kernels, shards(): pl.pallas_call(kernel, out_shape=jax.ShapeDtypeStruct(estimate.shape, F32...  72.5 us
    select_n x1, other arithmetic, shards(): return jnp.where(cells, estimate * (total / views), estimate)  2.4 us

profile of v4, /device:TPU:21, one launch (start us, length us, event | category | flops | bytes accessed | tf_op | source)
XLA Modules:
  0.0 75.8 jit_solution(4824051422302781014)
XLA Ops:
  0.0 0.7 broadcast_compare_fusion
  0.7 0.1 copy.7
  0.8 0.1 copy.8
  0.9 0.0 copy-start
  0.9 72.5 %deconvolve.1 = f32[16,64,256]{2,1,0:T(8,128)} custom-call(s32[4]{0:T(128)} %assign_ref.1, s32[3,16]{1,0:T(4,128)} %bitcast.7, f32[3,16,31]{2,1,0:T(8,128)} %bitcast.6, f32[16,64,256]{2,1,0:T(8,128)} %estimate.1, bf16[1,16,256,256]{3,2,1,0:T(8,128)(2,1)} %recorded_hbm.1), custom_call_target="tpu_custom_call" | custom-call | tf_op jit(solution)/shard_map/deconvolve/pallas_call | solution.py:342
  73.3 0.0 copy-done
  73.4 2.4 %multiply_select_fusion = f32[16,64,256]{2,1,0:T(8,128)} fusion(f32[16,64,256]{2,1,0:T(8,128)S(1)} %copy-done, f32[16,64,256]{2,1,0:T(8,128)} %deconvolve.1, pred[16,64]{1,0:T(8,128)(4,1)S(1)} %copy.8), kind=kLoop, calls=%fused_computation | loop fusion | flops 786432 | bytes 3146752 | tf_op jit(solution)/shard_map/jit(_where)/select_n | solution.py:371
  (2 shorter events, 0.0 us)
Async XLA Ops:
  0.9 72.5 %copy-start = (f32[16,64,256]{2,1,0:T(8,128)S(1)}, f32[16,64,256]{2,1,0:T(8,128)}, u32[]{:S(2)}) copy-start(f32[16,64,256]{2,1,0:T(8,128)} %estimate.1) | copy-start | bytes 3145732
